TPU v7x, 32 devices: a whole 2x2x4 slice. The times are simulated.
32 devices in a mesh: dp: 16 (over z, y, x), fsdp: 2 (over core).
Axes of the slice: x: 2, y: 2, z: 4, core: 2. Of those that a mesh axis runs over, the one named last changes fastest.
Arguments:
- tokens: bfloat16 [2, 18432, 1024], P(None, ('dp', 'fsdp')), may hold values from -6 to 6
- cotangent: bfloat16 [2, 18432, 1024], P(None, ('dp', 'fsdp')), may hold values from -6 to 6
- images: int32 [2, 16, 3], P(None, 'dp'), may hold values from 0 to 4, as said below
- attention_weight: float32 [4096, 1024], P(('dp', 'fsdp')), may hold values from -1 to 1
- attention_first: float32 [4096, 1024], P(('dp', 'fsdp')), may hold values from -0.00048828125 to 0.00048828125
- attention_second: float32 [4096, 1024], P(('dp', 'fsdp')), may hold values from 7.7838555e-11 to 3.1135422e-10
- widen_weight: float32 [1024, 5632], P(None, ('dp', 'fsdp')), may hold values from -0.1875 to 0.1875
- widen_first: float32 [1024, 5632], P(None, ('dp', 'fsdp')), may hold values from -0.00048828125 to 0.00048828125
- widen_second: float32 [1024, 5632], P(None, ('dp', 'fsdp')), may hold values from 7.7838555e-11 to 3.1135422e-10
- narrow_weight: float32 [2816, 1024], P(('dp', 'fsdp')), may hold values from -0.109375 to 0.109375
- narrow_first: float32 [2816, 1024], P(('dp', 'fsdp')), may hold values from -0.00048828125 to 0.00048828125
- narrow_second: float32 [2816, 1024], P(('dp', 'fsdp')), may hold values from 7.7838555e-11 to 3.1135422e-10
- norm_gains: float32 [2048], P(('dp', 'fsdp')), may hold values from 0.5 to 1.5
- gains_first: float32 [2048], P(('dp', 'fsdp')), may hold values from -0.0014648438 to 0.0014648438
- gains_second: float32 [2048], P(('dp', 'fsdp')), may hold values from 7.00547e-10 to 2.802188e-09
Outputs:
- block_output: float32 [2, 18432, 1024], P(None, ('dp', 'fsdp'))
- input_grad: float32 [2, 18432, 1024], P(None, ('dp', 'fsdp'))
- attention_master: float32 [4096, 1024], P(('dp', 'fsdp'))
- attention_mean: float32 [4096, 1024], P(('dp', 'fsdp'))
- attention_square: float32 [4096, 1024], P(('dp', 'fsdp'))
- widen_master: float32 [1024, 5632], P(None, ('dp', 'fsdp'))
- widen_mean: float32 [1024, 5632], P(None, ('dp', 'fsdp'))
- widen_square: float32 [1024, 5632], P(None, ('dp', 'fsdp'))
- narrow_master: float32 [2816, 1024], P(('dp', 'fsdp'))
- narrow_mean: float32 [2816, 1024], P(('dp', 'fsdp'))
- narrow_square: float32 [2816, 1024], P(('dp', 'fsdp'))
- gains_master: float32 [2048], P(('dp', 'fsdp'))
- gains_mean: float32 [2048], P(('dp', 'fsdp'))
- gains_square: float32 [2048], P(('dp', 'fsdp'))
- grad_norm: float32 [], replicated
Inputs may be any that keep to these rules, and one draw needn't show every extreme that they name: Each packed row's 3 slots are one of (4, 0, 0), (1, 1, 1), (2, 1, 0), (1, 2, 0): the images of the row's items in order, a 0 marking an empty slot.
All inputs are finite; a program needn't handle non-finite values.
Results may differ from a plain program's by a relative error of at most 0.014.
The roundings to bfloat16 on the way count: a program that leaves them out, or rounds other values in their place, can miss the bound.
Values may be sent and summed in bfloat16 or wider, within the bound.
A program may use at most 320 MiB of HBM per device.

v0:
```python
import jax
import jax.numpy as jnp
from jax import lax
from jax.sharding import PartitionSpec as P

HD = 64
TEXT = 128
PATCH = 256
ROW = 1152
NORM_EPS = 1e-06
MASKED = -1000000000.0
BETA_FIRST = 0.9
BETA_SECOND = 0.999
ADAM_EPS = 1e-08
MATRIX_RATE = 0.05
GAIN_RATE = 0.3
DECAY = 0.1
CLIP_LIMIT = 1.0
STEP_VALUE = 10.0


def gelu_tanh(values):
    return (
        0.5
        * values
        * (1.0 + jnp.tanh(0.7978845608028654 * (values + 0.044715 * values * values * values)))
    )


def gated_units(gate_pre, upward):
    return gelu_tanh(gate_pre) * upward


def rms_scale(values, gain_vector):
    return (
        values
        * lax.rsqrt(jnp.mean(values * values, axis=-1, keepdims=True) + NORM_EPS)
        * gain_vector
    )


def segment_ids(counts):
    item_sizes = jnp.where(counts > 0, TEXT + PATCH * counts, 0)
    item_ends = jnp.cumsum(item_sizes)
    places = jnp.arange(ROW, dtype=jnp.int32)
    return jnp.sum((places[:, None] >= item_ends[None, :]).astype(jnp.int32), axis=1)


def contract_rows(left, right):
    return lax.dot_general(
        left, right, (((0,), (0,)), ((), ())), preferred_element_type=jnp.float32
    )


def contract_cols(left, right):
    return lax.dot_general(
        left, right, (((1,), (1,)), ((), ())), preferred_element_type=jnp.float32
    )


def head_pairs(values):
    return values.reshape(values.shape[0], values.shape[1] // (2 * HD), 2 * HD).transpose(1, 0, 2)


def from_pairs(values):
    return values.transpose(1, 0, 2).reshape(values.shape[1], values.shape[0] * values.shape[2])


def flat_grads(grads):
    return (
        grads[0].reshape(-1, 128),
        grads[1].reshape(-1, 128),
        grads[2].reshape(-1, 128),
        grads[3],
    )


def shard_grads(reduced, model_width):
    widen_part = reduced[1].reshape(-1, model_width).T
    return (
        reduced[0].reshape(-1, model_width),
        widen_part,
        reduced[2].reshape(-1, model_width),
        reduced[3],
    )


def pair_forward(query_rows, key_rows, value_rows, same_item):
    query_heads = query_rows.reshape(query_rows.shape[0], 2, HD)
    key_heads = key_rows.reshape(key_rows.shape[0], 2, HD)
    value_heads = value_rows.reshape(value_rows.shape[0], 2, HD)
    scores = jnp.einsum("shd,khd->hsk", query_heads, key_heads, preferred_element_type=jnp.float32)
    scores = jnp.where(same_item[None], scores, MASKED)
    row_top = jnp.max(scores, axis=-1, keepdims=True)
    shifted = jnp.exp(scores - row_top)
    row_total = jnp.sum(shifted, axis=-1, keepdims=True)
    attend = shifted / row_total
    log_total = (row_top + jnp.log(row_total))[..., 0]
    mixed_heads = jnp.einsum(
        "hsk,khd->shd", attend.astype(jnp.bfloat16), value_heads, preferred_element_type=jnp.float32
    )
    return (mixed_heads.reshape(query_rows.shape[0], 2 * HD), log_total)


def pair_backward(query_rows, key_rows, value_rows, grad_rows, log_total, same_item):
    query_heads = query_rows.reshape(query_rows.shape[0], 2, HD)
    key_heads = key_rows.reshape(key_rows.shape[0], 2, HD)
    value_heads = value_rows.reshape(value_rows.shape[0], 2, HD)
    grad_heads = grad_rows.reshape(grad_rows.shape[0], 2, HD)
    scores = jnp.einsum("shd,khd->hsk", query_heads, key_heads, preferred_element_type=jnp.float32)
    scores = jnp.where(same_item[None], scores, MASKED)
    attend = jnp.exp(scores - log_total[..., None])
    grad_attend = jnp.einsum(
        "shd,khd->hsk", grad_heads, value_heads, preferred_element_type=jnp.float32
    )
    inner_sum = jnp.sum(attend * grad_attend, axis=-1, keepdims=True)
    grad_scores = (attend * (grad_attend - inner_sum)).astype(jnp.bfloat16)
    grad_query = jnp.einsum(
        "hsk,khd->shd", grad_scores, key_heads, preferred_element_type=jnp.float32
    )
    grad_key = jnp.einsum(
        "hsk,shd->khd", grad_scores, query_heads, preferred_element_type=jnp.float32
    )
    grad_value = jnp.einsum(
        "hsk,shd->khd", attend.astype(jnp.bfloat16), grad_heads, preferred_element_type=jnp.float32
    )
    query_count = query_rows.shape[0]
    key_count = key_rows.shape[0]
    return (
        grad_query.reshape(query_count, 2 * HD),
        grad_key.reshape(key_count, 2 * HD),
        grad_value.reshape(key_count, 2 * HD),
    )


def adam_update(master, first, second, gradient, factors, rate, decay):
    clip_factor, first_fix, second_fix = factors
    clipped = clip_factor * gradient
    first_new = BETA_FIRST * first + (1.0 - BETA_FIRST) * clipped
    second_new = BETA_SECOND * second + (1.0 - BETA_SECOND) * clipped * clipped
    master_new = master - rate * (
        first_new / first_fix / (jnp.sqrt(second_new / second_fix) + ADAM_EPS) + decay * master
    )
    return (master_new, first_new, second_new)


def local(
    tokens,
    cotangent,
    images,
    attention_weight,
    attention_first,
    attention_second,
    widen_weight,
    widen_first,
    widen_second,
    narrow_weight,
    narrow_first,
    narrow_second,
    norm_gains,
    gains_first,
    gains_second,
):
    model_width = tokens.shape[2]
    row_count = tokens.shape[1]
    hidden_width = narrow_weight.shape[0] * lax.axis_size(("dp", "fsdp"))
    half_index = lax.axis_index("fsdp")
    attention_low = attention_weight.astype(jnp.bfloat16)
    widen_low = widen_weight.astype(jnp.bfloat16)
    narrow_low = narrow_weight.astype(jnp.bfloat16)
    gains_low = norm_gains.astype(jnp.bfloat16)

    def forward(full_weights, rows_in, same_item):
        attention_full, widen_full, narrow_full, gains_full = full_weights
        matrices = attention_full.reshape(4, model_width, model_width)
        first_gain = gains_full[:model_width].astype(jnp.float32)
        second_gain = gains_full[model_width:].astype(jnp.float32)
        inputs = rows_in.astype(jnp.float32)
        normed = rms_scale(inputs, first_gain).astype(jnp.bfloat16)
        projected = jnp.einsum(
            "sd,jde->jse", normed, matrices[:3], preferred_element_type=jnp.float32
        ).astype(jnp.bfloat16)
        keys_all, values_all = (
            lax.all_gather(projected[1], "fsdp", axis=0, tiled=True),
            lax.all_gather(projected[2], "fsdp", axis=0, tiled=True),
        )
        mixed_heads, log_total = lax.map(
            lambda pieces: pair_forward(pieces[0], pieces[1], pieces[2], same_item),
            (head_pairs(projected[0]), head_pairs(keys_all), head_pairs(values_all)),
        )
        mixed_heads = from_pairs(mixed_heads).astype(jnp.bfloat16)
        hidden_one = inputs + jnp.dot(mixed_heads, matrices[3], preferred_element_type=jnp.float32)
        second = rms_scale(hidden_one, second_gain).astype(jnp.bfloat16)
        widened = jnp.dot(second, widen_full, preferred_element_type=jnp.float32)
        gate_pre = widened[:, :hidden_width]
        upward = widened[:, hidden_width:]
        hidden = gated_units(gate_pre, upward).astype(jnp.bfloat16)
        result = hidden_one + jnp.dot(hidden, narrow_full, preferred_element_type=jnp.float32)
        saved = (
            inputs,
            normed,
            projected[0],
            keys_all,
            values_all,
            log_total,
            mixed_heads,
            hidden_one,
            second,
            gate_pre,
            upward,
            hidden,
        )
        return (result, saved)

    def backward(full_weights, saved, grad_rows, same_item):
        attention_full, widen_full, narrow_full, gains_full = full_weights
        matrices = attention_full.reshape(4, model_width, model_width)
        first_gain = gains_full[:model_width].astype(jnp.float32)
        second_gain = gains_full[model_width:].astype(jnp.float32)
        (
            inputs,
            normed,
            query_rows,
            keys_all,
            values_all,
            log_total,
            mixed_heads,
            hidden_one,
            second,
            gate_pre,
            upward,
            hidden,
        ) = saved
        grad_narrow = contract_rows(hidden, grad_rows)
        grad_hidden = contract_cols(grad_rows, narrow_full)
        unused_value, gated_back = jax.vjp(gated_units, gate_pre, upward)
        grad_gate, grad_up = gated_back(grad_hidden)
        grad_widened = jnp.concatenate([grad_gate, grad_up], axis=1).astype(jnp.bfloat16)
        grad_widen_cols = contract_rows(grad_widened, second)
        grad_second = contract_cols(grad_widened, widen_full)
        unused_norm, second_back = jax.vjp(rms_scale, hidden_one, second_gain)
        grad_from_norm, grad_gain_two = second_back(grad_second)
        grad_hidden_one = grad_rows.astype(jnp.float32) + grad_from_norm
        grad_branch = grad_hidden_one.astype(jnp.bfloat16)
        grad_output_proj = contract_rows(mixed_heads, grad_branch)
        grad_mixed = contract_cols(grad_branch, matrices[3]).astype(jnp.bfloat16)
        grad_query, grad_key, grad_value = lax.map(
            lambda pieces: pair_backward(
                pieces[0], pieces[1], pieces[2], pieces[3], pieces[4], same_item
            ),
            (
                head_pairs(query_rows),
                head_pairs(keys_all),
                head_pairs(values_all),
                head_pairs(grad_mixed),
                log_total,
            ),
        )
        own_key, own_value = (
            lax.psum_scatter(
                from_pairs(grad_key).astype(jnp.bfloat16), "fsdp", scatter_dimension=0, tiled=True
            ).astype(jnp.float32),
            lax.psum_scatter(
                from_pairs(grad_value).astype(jnp.bfloat16), "fsdp", scatter_dimension=0, tiled=True
            ).astype(jnp.float32),
        )
        grad_projected = jnp.stack([from_pairs(grad_query), own_key, own_value]).astype(
            jnp.bfloat16
        )
        grad_qkv = jnp.einsum(
            "sd,jse->jde", normed, grad_projected, preferred_element_type=jnp.float32
        )
        grad_normed = jnp.einsum(
            "jse,jde->sd", grad_projected, matrices[:3], preferred_element_type=jnp.float32
        )
        unused_first, first_back = jax.vjp(rms_scale, inputs, first_gain)
        grad_from_first, grad_gain_one = first_back(grad_normed)
        input_rows = grad_hidden_one + grad_from_first
        grad_attention = jnp.concatenate([grad_qkv, grad_output_proj[None]], axis=0).reshape(
            4 * model_width, model_width
        )
        grad_gains = jnp.concatenate([grad_gain_one, grad_gain_two])
        return (input_rows, (grad_attention, grad_widen_cols, grad_narrow, grad_gains))

    start_grads = (
        jnp.zeros((4 * model_width, model_width), jnp.float32),
        jnp.zeros((2 * hidden_width, model_width), jnp.float32),
        jnp.zeros((hidden_width, model_width), jnp.float32),
        jnp.zeros((2 * model_width,), jnp.float32),
    )

    def micro_step(running, pieces):
        rows_in, grad_rows, counts = pieces
        seg_full = segment_ids(counts)
        seg_own = lax.dynamic_slice_in_dim(seg_full, half_index * row_count, row_count)
        same_item = seg_own[:, None] == seg_full[None, :]
        forward_weights = (
            lax.all_gather(attention_low, ("dp", "fsdp"), axis=0, tiled=True),
            lax.all_gather(widen_low, ("dp", "fsdp"), axis=1, tiled=True),
            lax.all_gather(narrow_low, ("dp", "fsdp"), axis=0, tiled=True),
            lax.all_gather(gains_low, ("dp", "fsdp"), axis=0, tiled=True),
        )
        result, saved = forward(forward_weights, rows_in, same_item)
        backward_weights = (
            lax.all_gather(attention_low, ("dp", "fsdp"), axis=0, tiled=True),
            lax.all_gather(widen_low, ("dp", "fsdp"), axis=1, tiled=True),
            lax.all_gather(narrow_low, ("dp", "fsdp"), axis=0, tiled=True),
            lax.all_gather(gains_low, ("dp", "fsdp"), axis=0, tiled=True),
        )
        input_rows, gradients = backward(backward_weights, saved, grad_rows, same_item)
        running = tuple((total + fresh for total, fresh in zip(running, gradients)))
        return (running, (result, input_rows))

    totals, (block_output, input_grad) = lax.scan(
        micro_step, start_grads, (tokens, cotangent, images[:, 0, :])
    )
    flat_list = flat_grads(totals)
    summed = (
        lax.psum_scatter(flat_list[0], ("dp", "fsdp"), scatter_dimension=0, tiled=True),
        lax.psum_scatter(flat_list[1], ("dp", "fsdp"), scatter_dimension=0, tiled=True),
        lax.psum_scatter(flat_list[2], ("dp", "fsdp"), scatter_dimension=0, tiled=True),
        lax.psum_scatter(flat_list[3], ("dp", "fsdp"), scatter_dimension=0, tiled=True),
    )
    reduced = shard_grads(summed, model_width)
    local_squares = (
        jnp.sum(reduced[0] * reduced[0])
        + jnp.sum(reduced[1] * reduced[1])
        + jnp.sum(reduced[2] * reduced[2])
        + jnp.sum(reduced[3] * reduced[3])
    )
    grad_norm = jnp.sqrt(lax.psum(local_squares, ("dp", "fsdp")))
    clip_factor = jnp.minimum(1.0, CLIP_LIMIT / (grad_norm + 1e-06))
    step_value = jnp.float32(STEP_VALUE)
    factors = (
        clip_factor,
        1.0 - jnp.power(jnp.float32(BETA_FIRST), step_value),
        1.0 - jnp.power(jnp.float32(BETA_SECOND), step_value),
    )
    attention_master, attention_mean, attention_square = adam_update(
        attention_weight, attention_first, attention_second, reduced[0], factors, MATRIX_RATE, DECAY
    )
    widen_master, widen_mean, widen_square = adam_update(
        widen_weight, widen_first, widen_second, reduced[1], factors, MATRIX_RATE, DECAY
    )
    narrow_master, narrow_mean, narrow_square = adam_update(
        narrow_weight, narrow_first, narrow_second, reduced[2], factors, MATRIX_RATE, DECAY
    )
    gains_master, gains_mean, gains_square = adam_update(
        norm_gains, gains_first, gains_second, reduced[3], factors, GAIN_RATE, 0.0
    )
    return (
        block_output,
        input_grad,
        attention_master,
        attention_mean,
        attention_square,
        widen_master,
        widen_mean,
        widen_square,
        narrow_master,
        narrow_mean,
        narrow_square,
        gains_master,
        gains_mean,
        gains_square,
        grad_norm,
    )


def solution(mesh):
    placed = (
        P(None, ("dp", "fsdp"), None),
        P(None, ("dp", "fsdp"), None),
        P(None, "dp", None),
        P(("dp", "fsdp"), None),
        P(("dp", "fsdp"), None),
        P(("dp", "fsdp"), None),
        P(None, ("dp", "fsdp")),
        P(None, ("dp", "fsdp")),
        P(None, ("dp", "fsdp")),
        P(("dp", "fsdp"), None),
        P(("dp", "fsdp"), None),
        P(("dp", "fsdp"), None),
        P(("dp", "fsdp")),
        P(("dp", "fsdp")),
        P(("dp", "fsdp")),
    )
    return jax.shard_map(
        local,
        mesh=mesh,
        in_specs=placed,
        out_specs=(
            P(None, ("dp", "fsdp"), None),
            P(None, ("dp", "fsdp"), None),
            P(("dp", "fsdp"), None),
            P(("dp", "fsdp"), None),
            P(("dp", "fsdp"), None),
            P(None, ("dp", "fsdp")),
            P(None, ("dp", "fsdp")),
            P(None, ("dp", "fsdp")),
            P(("dp", "fsdp"), None),
            P(("dp", "fsdp"), None),
            P(("dp", "fsdp"), None),
            P(("dp", "fsdp")),
            P(("dp", "fsdp")),
            P(("dp", "fsdp")),
            P(),
        ),
        check_vma=False,
    )
```

profile of v0, /device:TPU:0, one launch (start us, length us, event | category | flops | bytes accessed | tf_op | source)
XLA Modules:
  0.0 1677.6 jit_solution(11807096123481081183)
XLA Ops:
  12.5 999.1 %while.73 = (s32[]{:T(128)}, f32[4096,1024]{1,0:T(8,128)}, f32[5632,1024]{1,0:T(8,128)}, f32[2816,1024]{1,0:T(8,128)}, f32[2048]{0:T(1024)}, /*index=5*/f32[2,57...) while((s32[]{:T(128)}, f32[4096,1024]{1,0:T(8,128)}, ...), condition=%wide.region_18.19_spmd.clone, body=%wide.region_0.18_spmd.clone.sunk | while | flops 45746876416 | bytes 740799360 | solution.py:314
  14.2 42.5 %all-reduce.4 = bf16[2048]{0:T(1024)(128)(2,1)S(1)} all-reduce(bf16[2048]{0:T(1024)(128)(2,1)S(1)} %dynamic-update-slice.3), channel_id=1, replica_groups=mesh['dp'=16,'fsdp'=2] {'dp','fsdp'}, use_global_device_ids=true, to_apply=%add | all-reduce | flops 2048 | bytes 8192 | tf_op jit(solution)/shard_map/while
  58.4 39.4 %all-gather.14.cloned.1.call-done = bf16[4096,1024]{1,0:T(8,128)(2,1)} async-done(((bf16[128,1024]{1,0:T(8,128)(2,1)}), bf16[4096,1024]{1,0:T(8,128)(2,1)}) %all-gather.14.cloned.1.call-update) | async-done | bytes 8388624 | tf_op jit(solution)/shard_map/while/body/eval_jaxpr/all_gather | solution.py:298
  120.1 10.7 all-gather.18.cloned.1.call-done
  136.3 59.2 %while.74 = (s32[]{:T(128)}, bf16[8,576,128]{1,2,0:T(8,128)(2,1)}, f32[8,2,576]{2,1,0:T(2,128)}, bf16[8,1152,128]{1,2,0:T(8,128)(2,1)S(1)}, bf16[8,576,128]{1,2,...) while((s32[]{:T(128)}, bf16[8,576,128]{1,2,0:T(8,128)(2,1)}, ...), condition=%wide.region_7.7_spmd.clone, body=%wide.region_4.6_spmd.clone.sunk | while | flops 349690752 | bytes 19968356 | solution.py:187
  200.8 25.7 %all-gather.20.cloned.1.call-done = bf16[1024,5632]{0,1:T(8,128)(2,1)} async-done(((bf16[1024,176]{0,1:T(8,128)(2,1)}), bf16[1024,5632]{0,1:T(8,128)(2,1)}) %all-gather.20.cloned.1.call-update) | async-done | bytes 11534352 | tf_op jit(solution)/shard_map/while/body/eval_jaxpr/all_gather | solution.py:299
  226.5 13.3 fusion.176
  239.8 55.6 %all-gather.22.cloned.1.call-done = bf16[2816,1024]{1,0:T(8,128)(2,1)} async-done(((bf16[88,1024]{1,0:T(8,128)(2,1)}), bf16[2816,1024]{1,0:T(8,128)(2,1)}) %all-gather.22.cloned.1.call-update) | async-done | bytes 5767184 | tf_op jit(solution)/shard_map/while/body/eval_jaxpr/all_gather | solution.py:307
  295.4 16.1 fusion.177
  311.5 13.0 multiply_reduce_fusion.12
  332.4 90.6 %while.75 = (s32[]{:T(128)}, bf16[8,576,128]{1,2,0:T(8,128)(2,1)}, bf16[8,1152,128]{1,2,0:T(8,128)(2,1)}, bf16[8,1152,128]{1,2,0:T(8,128)(2,1)}, bf16[8,1152,128...) while((s32[]{:T(128)}, bf16[8,576,128]{1,2,0:T(8,128)(2,1)}, ...), condition=%wide.region_12.12_spmd.clone, body=%wide.region_10.11_spmd.clone.sunk | while | flops 860625792 | bytes 46643592 | solution.py:247
  456.1 16.1 select_add_fusion.4
  492.2 10.9 bitcast_add_fusion.2
  507.7 40.3 %all-reduce.4 = bf16[2048]{0:T(1024)(128)(2,1)S(1)} all-reduce(bf16[2048]{0:T(1024)(128)(2,1)S(1)} %dynamic-update-slice.3), channel_id=1, replica_groups=mesh['dp'=16,'fsdp'=2] {'dp','fsdp'}, use_global_device_ids=true, to_apply=%add | all-reduce | flops 2048 | bytes 8192 | tf_op jit(solution)/shard_map/while
  549.7 38.0 %all-gather.14.cloned.1.call-done = bf16[4096,1024]{1,0:T(8,128)(2,1)} async-done(((bf16[128,1024]{1,0:T(8,128)(2,1)}), bf16[4096,1024]{1,0:T(8,128)(2,1)}) %all-gather.14.cloned.1.call-update) | async-done | bytes 8388624 | tf_op jit(solution)/shard_map/while/body/eval_jaxpr/all_gather | solution.py:298
  626.0 59.2 %while.74 = (s32[]{:T(128)}, bf16[8,576,128]{1,2,0:T(8,128)(2,1)}, f32[8,2,576]{2,1,0:T(2,128)}, bf16[8,1152,128]{1,2,0:T(8,128)(2,1)S(1)}, bf16[8,576,128]{1,2,...) while((s32[]{:T(128)}, bf16[8,576,128]{1,2,0:T(8,128)(2,1)}, ...), condition=%wide.region_7.7_spmd.clone, body=%wide.region_4.6_spmd.clone.sunk | while | flops 349690752 | bytes 19968356 | solution.py:187
  690.5 25.9 %all-gather.20.cloned.1.call-done = bf16[1024,5632]{0,1:T(8,128)(2,1)} async-done(((bf16[1024,176]{0,1:T(8,128)(2,1)}), bf16[1024,5632]{0,1:T(8,128)(2,1)}) %all-gather.20.cloned.1.call-update) | async-done | bytes 11534352 | tf_op jit(solution)/shard_map/while/body/eval_jaxpr/all_gather | solution.py:299
  716.4 13.3 fusion.176
  729.7 55.6 %all-gather.22.cloned.1.call-done = bf16[2816,1024]{1,0:T(8,128)(2,1)} async-done(((bf16[88,1024]{1,0:T(8,128)(2,1)}), bf16[2816,1024]{1,0:T(8,128)(2,1)}) %all-gather.22.cloned.1.call-update) | async-done | bytes 5767184 | tf_op jit(solution)/shard_map/while/body/eval_jaxpr/all_gather | solution.py:307
  785.2 16.4 fusion.177
  801.7 13.0 multiply_reduce_fusion.12
  822.6 90.5 %while.75 = (s32[]{:T(128)}, bf16[8,576,128]{1,2,0:T(8,128)(2,1)}, bf16[8,1152,128]{1,2,0:T(8,128)(2,1)}, bf16[8,1152,128]{1,2,0:T(8,128)(2,1)}, bf16[8,1152,128...) while((s32[]{:T(128)}, bf16[8,576,128]{1,2,0:T(8,128)(2,1)}, ...), condition=%wide.region_12.12_spmd.clone, body=%wide.region_10.11_spmd.clone.sunk | while | flops 860625792 | bytes 46643592 | solution.py:247
  948.8 22.0 %select_add_fusion.4 = f32[5632,1024]{1,0:T(8,128)} fusion(f32[5632,1024]{1,0:T(8,128)} %get-tuple-element.887, pred[]{:T(512)S(6)} %compare.3, bf16[576,2816]{1,0:T(8,128)(2,1)} %copy-done.44, bf16[576,2816]{1,0:T(8,128)(2,1)} %copy-done.43, f32[576,1024]{1,0:T(8,128)S(1)} %copy-done.6, f32[1024]{0:T(1024)S(1)} %get-tuple-element.758, ...), kind=kOutput, calls=%fused_computation.27.clone.1 | convolution fusion | flops 6670057472 | bytes 54991104 | tf_op jit(solution)/shard_map/while/body/eval_jaxpr/dot_general | solution.py:50
  990.8 14.0 bitcast_add_fusion.2
  1011.6 13.3 reshape.263
  1025.0 18.1 %reshape.261 = f32[32768,128]{1,0:T(8,128)} reshape(f32[4096,1024]{1,0:T(8,128)} %get-tuple-element.288) | data formatting | bytes 33554432 | tf_op jit(solution)/shard_map/reshape | solution.py:71
  1043.1 24.6 %reshape.262 = f32[45056,128]{1,0:T(8,128)} reshape(f32[5632,1024]{1,0:T(8,128)} %get-tuple-element.289) | data formatting | bytes 46137344 | tf_op jit(solution)/shard_map/reshape | solution.py:72
  1068.5 42.4 %all-reduce.2 = f32[2048]{0:T(1024)S(1)} all-reduce(f32[2048]{0:T(1024)S(1)} %copy-done.34), channel_id=9, replica_groups=mesh['dp'=16,'fsdp'=2] {'dp','fsdp'}, use_global_device_ids=true, to_apply=%region_25.26.clone | all-reduce | flops 2048 | bytes 16384
  1111.5 67.6 %reduce-scatter.10.cloned.1.call-done = f32[704,128]{1,0:T(8,128)} async-done(((f32[22528,128]{1,0:T(8,128)}), f32[704,128]{1,0:T(8,128)}) %reduce-scatter.10.cloned.1.call-update) | async-done | bytes 360464 | tf_op jit(solution)/shard_map/reduce_scatter | solution.py:321
  1180.7 179.4 %reduce-scatter.6.cloned.1.call-done = f32[1024,128]{1,0:T(8,128)} async-done(((f32[32768,128]{1,0:T(8,128)}), f32[1024,128]{1,0:T(8,128)}) %reduce-scatter.6.cloned.1.call-update) | async-done | bytes 524304 | tf_op jit(solution)/shard_map/reduce_scatter | solution.py:319
  1361.9 248.2 %reduce-scatter.8.cloned.1.call-done = f32[1408,128]{1,0:T(8,128)} async-done(((f32[45056,128]{1,0:T(8,128)}), f32[1408,128]{1,0:T(8,128)}) %reduce-scatter.8.cloned.1.call-update) | async-done | bytes 720912 | tf_op jit(solution)/shard_map/reduce_scatter | solution.py:320
  1614.7 44.6 %psum.7 = f32[]{:T(128)} all-reduce(f32[]{:T(128)S(6)} %add.212), channel_id=1, replica_groups=mesh['dp'=16,'fsdp'=2] {'dp','fsdp'}, use_global_device_ids=true, to_apply=%region_27.28 | all-reduce | flops 1 | bytes 8 | tf_op jit(solution)/shard_map/psum | solution.py:331
  (649 shorter events, 530.1 us)
Async XLA Ops:
  12.5 88.7 %copy-start.10 = (bf16[1024,176]{0,1:T(8,128)(2,1)}, bf16[1024,176]{0,1:T(8,128)(2,1)S(1)}, u32[]{:S(2)}) copy-start(bf16[1024,176]{0,1:T(8,128)(2,1)S(1)} %get-tuple-element.921) | copy-start | bytes 1081348 | tf_op jit(solution)/shard_map/while
  12.5 88.7 %copy-start.14 = (bf16[88,1024]{1,0:T(8,128)(2,1)}, bf16[88,1024]{1,0:T(8,128)(2,1)S(1)}, u32[]{:S(2)}) copy-start(bf16[88,1024]{1,0:T(8,128)(2,1)S(1)} %get-tuple-element.922) | copy-start | bytes 540676 | tf_op jit(solution)/shard_map/while
  12.5 85.2 %all-gather.14.cloned.1.call-start = ((), (), s32[]{:S(2)}) async-start(), calls=%async_computation.8 | async-start | bytes 8650752 | tf_op jit(solution)/shard_map/while/body/eval_jaxpr/all_gather | solution.py:298
  13.3 103.9 %all-gather.16.cloned.1.call-start = ((), (), s32[]{:S(2)}) async-start(), calls=%async_computation.9 | async-start | bytes 3538944 | tf_op jit(solution)/shard_map/while/body/eval_jaxpr/all_gather | solution.py:185
  58.3 42.9 %copy-start.20 = (f32[576]{0:T(1024)}, f32[576]{0:T(1024)S(1)}, u32[]{:S(2)}) copy-start(f32[576]{0:T(1024)S(1)} %fusion.171) | copy-start | bytes 6916 | tf_op jit(solution)/shard_map/while
  58.3 42.9 %copy-start.28 = (f32[576]{0:T(1024)}, f32[576]{0:T(1024)S(1)}, u32[]{:S(2)}) copy-start(f32[576]{0:T(1024)S(1)} %fusion.172) | copy-start | bytes 6916 | tf_op jit(solution)/shard_map/while
  58.4 42.9 %copy-start.26 = (f32[1024]{0:T(1024)}, f32[1024]{0:T(1024)S(1)}, u32[]{:S(2)}) copy-start(f32[1024]{0:T(1024)S(1)} %get-tuple-element.750) | copy-start | bytes 12292 | tf_op jit(solution)/shard_map/while
  58.4 42.9 %copy-start.3 = (bf16[2,576,1024]{2,1,0:T(8,128)(2,1)S(1)}, bf16[2,576,1024]{2,1,0:T(8,128)(2,1)}, u32[]{:S(2)}) copy-start(bf16[2,576,1024]{2,1,0:T(8,128)(2,1)} %get-tuple-element.915) | copy-start | bytes 7077892 | tf_op jit(solution)/shard_map/while
  107.4 23.4 %all-gather.18.cloned.1.call-start = ((), (), s32[]{:S(2)}) async-start(), calls=%async_computation.10 | async-start | bytes 3538944 | tf_op jit(solution)/shard_map/while/body/eval_jaxpr/all_gather | solution.py:184
  108.2 118.3 %all-gather.20.cloned.1.call-start = ((), (), s32[]{:S(2)}) async-start(), calls=%async_computation.11 | async-start | bytes 11894784 | tf_op jit(solution)/shard_map/while/body/eval_jaxpr/all_gather | solution.py:299
  108.7 186.7 %all-gather.22.cloned.1.call-start = ((), (), s32[]{:S(2)}) async-start(), calls=%async_computation.12 | async-start | bytes 5947392 | tf_op jit(solution)/shard_map/while/body/eval_jaxpr/all_gather | solution.py:307
  109.3 362.9 %reduce-scatter.12.cloned.1.call-start = ((), (), s32[]{:S(2)}) async-start(), calls=%async_computation.13 | async-start | bytes 3538944 | tf_op jit(solution)/shard_map/while/body/eval_jaxpr/reduce_scatter | solution.py:263
  200.8 123.8 %copy-start.30 = (f32[576]{0:T(1024)}, f32[576]{0:T(1024)S(1)}, u32[]{:S(2)}) copy-start(f32[576]{0:T(1024)S(1)} %fusion.175) | copy-start | bytes 6916 | tf_op jit(solution)/shard_map/while
  427.3 44.9 %reduce-scatter.14.cloned.1.call-start = ((), (), s32[]{:S(2)}) async-start(), calls=%async_computation.14 | async-start | bytes 3538944 | tf_op jit(solution)/shard_map/while/body/eval_jaxpr/reduce_scatter | solution.py:260
  506.0 85.1 %copy-start.10 = (bf16[1024,176]{0,1:T(8,128)(2,1)}, bf16[1024,176]{0,1:T(8,128)(2,1)S(1)}, u32[]{:S(2)}) copy-start(bf16[1024,176]{0,1:T(8,128)(2,1)S(1)} %get-tuple-element.921) | copy-start | bytes 1081348 | tf_op jit(solution)/shard_map/while
  506.0 85.1 %copy-start.14 = (bf16[88,1024]{1,0:T(8,128)(2,1)}, bf16[88,1024]{1,0:T(8,128)(2,1)S(1)}, u32[]{:S(2)}) copy-start(bf16[88,1024]{1,0:T(8,128)(2,1)S(1)} %get-tuple-element.922) | copy-start | bytes 540676 | tf_op jit(solution)/shard_map/while
  506.0 81.6 %all-gather.14.cloned.1.call-start = ((), (), s32[]{:S(2)}) async-start(), calls=%async_computation.8 | async-start | bytes 8650752 | tf_op jit(solution)/shard_map/while/body/eval_jaxpr/all_gather | solution.py:298
  506.8 100.2 %all-gather.16.cloned.1.call-start = ((), (), s32[]{:S(2)}) async-start(), calls=%async_computation.9 | async-start | bytes 3538944 | tf_op jit(solution)/shard_map/while/body/eval_jaxpr/all_gather | solution.py:185
  549.6 41.5 %copy-start.20 = (f32[576]{0:T(1024)}, f32[576]{0:T(1024)S(1)}, u32[]{:S(2)}) copy-start(f32[576]{0:T(1024)S(1)} %fusion.171) | copy-start | bytes 6916 | tf_op jit(solution)/shard_map/while
  549.6 41.5 %copy-start.28 = (f32[576]{0:T(1024)}, f32[576]{0:T(1024)S(1)}, u32[]{:S(2)}) copy-start(f32[576]{0:T(1024)S(1)} %fusion.172) | copy-start | bytes 6916 | tf_op jit(solution)/shard_map/while
  549.6 41.5 %copy-start.26 = (f32[1024]{0:T(1024)}, f32[1024]{0:T(1024)S(1)}, u32[]{:S(2)}) copy-start(f32[1024]{0:T(1024)S(1)} %get-tuple-element.750) | copy-start | bytes 12292 | tf_op jit(solution)/shard_map/while
  597.3 23.3 %all-gather.18.cloned.1.call-start = ((), (), s32[]{:S(2)}) async-start(), calls=%async_computation.10 | async-start | bytes 3538944 | tf_op jit(solution)/shard_map/while/body/eval_jaxpr/all_gather | solution.py:184
  597.9 118.5 %all-gather.20.cloned.1.call-start = ((), (), s32[]{:S(2)}) async-start(), calls=%async_computation.11 | async-start | bytes 11894784 | tf_op jit(solution)/shard_map/while/body/eval_jaxpr/all_gather | solution.py:299
  598.6 186.6 %all-gather.22.cloned.1.call-start = ((), (), s32[]{:S(2)}) async-start(), calls=%async_computation.12 | async-start | bytes 5947392 | tf_op jit(solution)/shard_map/while/body/eval_jaxpr/all_gather | solution.py:307
  599.2 371.6 %reduce-scatter.12.cloned.1.call-start = ((), (), s32[]{:S(2)}) async-start(), calls=%async_computation.13 | async-start | bytes 3538944 | tf_op jit(solution)/shard_map/while/body/eval_jaxpr/reduce_scatter | solution.py:263
  690.5 124.3 %copy-start.30 = (f32[576]{0:T(1024)}, f32[576]{0:T(1024)S(1)}, u32[]{:S(2)}) copy-start(f32[576]{0:T(1024)S(1)} %fusion.175) | copy-start | bytes 6916 | tf_op jit(solution)/shard_map/while
  917.4 53.4 %reduce-scatter.14.cloned.1.call-start = ((), (), s32[]{:S(2)}) async-start(), calls=%async_computation.14 | async-start | bytes 3538944 | tf_op jit(solution)/shard_map/while/body/eval_jaxpr/reduce_scatter | solution.py:260
  1011.6 167.5 %reduce-scatter.10.cloned.1.call-start = ((), (), s32[]{:S(2)}) async-start(), calls=%async_computation.7 | async-start | bytes 11894784 | tf_op jit(solution)/shard_map/reduce_scatter | solution.py:321
  1025.0 335.1 %reduce-scatter.6.cloned.1.call-start = ((), (), s32[]{:S(2)}) async-start(), calls=%async_computation.5 | async-start | bytes 17301504 | tf_op jit(solution)/shard_map/reduce_scatter | solution.py:319
  1043.1 567.0 %reduce-scatter.8.cloned.1.call-start = ((), (), s32[]{:S(2)}) async-start(), calls=%async_computation.6 | async-start | bytes 23789568 | tf_op jit(solution)/shard_map/reduce_scatter | solution.py:320
  1361.9 300.1 %copy-start.19 = (f32[1024,128]{1,0:T(8,128)S(1)}, f32[1024,128]{1,0:T(8,128)}, u32[]{:S(2)}) copy-start(f32[1024,128]{1,0:T(8,128)} %reduce-scatter.6.cloned.1.call-done) | copy-start | bytes 1572868
  1610.1 51.7 %copy-start.17 = (f32[1408,128]{1,0:T(8,128)S(1)}, f32[1408,128]{1,0:T(8,128)}, u32[]{:S(2)}) copy-start(f32[1408,128]{1,0:T(8,128)} %reduce-scatter.8.cloned.1.call-done) | copy-start | bytes 2162692
  (63 other events, 467.1 us)
Sparse Core Ops, SparseCore 0:
  16.8 80.9 all-gather.13
  107.5 9.5 all-gather.15
  118.7 12.1 all-gather.17
  134.1 92.3 all-gather.19
  229.8 65.6 all-gather.21
  427.5 8.8 reduce-scatter.11
  438.7 11.0 reduce-scatter.13
  510.3 77.2 all-gather.13
  597.4 9.5 all-gather.15
  608.4 12.1 all-gather.17
  624.0 92.3 all-gather.19
  719.6 65.5 all-gather.21
  917.5 8.8 reduce-scatter.11
  928.6 11.0 reduce-scatter.13
Sparse Core Ops, SparseCore 1:
  1025.0 154.0 reduce-scatter.9
  1181.2 178.8 reduce-scatter.5
  1362.3 247.8 reduce-scatter.7
where the time goes:
time: 1680 us
  waiting for transfers between devices  772 us (46%)
  matrix products  350 us (21%)
  local copies, waits for them, and re-layouts  247 us (15%)
  blocking collectives  170 us (10%)
  other arithmetic  110 us (7%)
  between operations  20.4 us (1%)
    reduce_scatter x1, waiting for transfers between devices, local(): lax.psum_scatter(flat_list[1], ('dp', 'fsdp'), scatter_dimension=0, tiled...  248 us
    reduce_scatter x1, waiting for transfers between devices, local(): lax.psum_scatter(flat_list[0], ('dp', 'fsdp'), scatter_dimension=0, tiled...  179 us
    all_gather x2, waiting for transfers between devices, micro_step(): lax.all_gather(narrow_low, ('dp', 'fsdp'), axis=0, tiled=True)  111 us
    while x2, blocking collectives  82.8 us
    dynamic_slice x96, local copies, waits for them, and re-layouts, forward(): lax.map(lambda pieces: pair_forward(pieces[0], pieces[1], pieces[2], same...  77.6 us
    all_gather x2, waiting for transfers between devices, micro_step(): lax.all_gather(attention_low, ('dp', 'fsdp'), axis=0, tiled=True)  77.3 us
    reduce_scatter x1, waiting for transfers between devices, local(): lax.psum_scatter(flat_list[2], ('dp', 'fsdp'), scatter_dimension=0, tiled...  67.6 us
    dot_general x6, matrix products, contract_rows(): lax.dot_general(left, right, (((0,), (0,)), ((), ())), preferred_element_...  66.5 us
  transfers between devices with their start and end apart: 17, of which 13 were waited for; matrix products, arithmetic and copies ran while one was open for 19% of the time, Pallas kernels for 0%

commit v1 on v0

--- a/solution.py
+++ b/solution.py
@@ -328,7 +328,7 @@
         + jnp.sum(reduced[2] * reduced[2])
         + jnp.sum(reduced[3] * reduced[3])
     )
-    grad_norm = jnp.sqrt(lax.psum(local_squares, ("dp", "fsdp")))
+    grad_norm = jnp.sqrt(lax.psum(lax.psum(local_squares, "fsdp"), "dp"))
     clip_factor = jnp.minimum(1.0, CLIP_LIMIT / (grad_norm + 1e-06))
     step_value = jnp.float32(STEP_VALUE)
     factors = (

time: 1680 us -> 1690 us (level)
    psum x1 -> x2, blocking collectives: 44.6 us -> 49.6 us  [local(): grad_norm = jnp.sqrt(lax.psum(lax.psum(local_squares, 'fsdp'), 'dp'))]
where the time goes in v1:
time: 1690 us; the launch traced here: 1680 us
  waiting for transfers between devices  772 us (46%)
  matrix products  350 us (21%)
  local copies, waits for them, and re-layouts  247 us (15%)
  blocking collectives  175 us (10%)
  other arithmetic  110 us (7%)
  between operations  20.4 us (1%)
    reduce_scatter x1, waiting for transfers between devices, local(): lax.psum_scatter(flat_list[1], ('dp', 'fsdp'), scatter_dimension=0, tiled...  248 us
    reduce_scatter x1, waiting for transfers between devices, local(): lax.psum_scatter(flat_list[0], ('dp', 'fsdp'), scatter_dimension=0, tiled...  179 us
    all_gather x2, waiting for transfers between devices, micro_step(): lax.all_gather(narrow_low, ('dp', 'fsdp'), axis=0, tiled=True)  111 us
    while x2, blocking collectives  82.8 us
    dynamic_slice x96, local copies, waits for them, and re-layouts, forward(): lax.map(lambda pieces: pair_forward(pieces[0], pieces[1], pieces[2], same...  77.6 us
    all_gather x2, waiting for transfers between devices, micro_step(): lax.all_gather(attention_low, ('dp', 'fsdp'), axis=0, tiled=True)  77.3 us
    reduce_scatter x1, waiting for transfers between devices, local(): lax.psum_scatter(flat_list[2], ('dp', 'fsdp'), scatter_dimension=0, tiled...  67.2 us
    dot_general x6, matrix products, contract_rows(): lax.dot_general(left, right, (((0,), (0,)), ((), ())), preferred_element_...  66.5 us
  transfers between devices with their start and end apart: 17, of which 13 were waited for; matrix products, arithmetic and copies ran while one was open for 19% of the time, Pallas kernels for 0%

profile of v1, /device:TPU:0, one launch (start us, length us, event | category | flops | bytes accessed | tf_op | source)
XLA Modules:
  0.0 1682.6 jit_solution(1974041498694560275)
XLA Ops:
  12.5 999.2 %while.73 = (s32[]{:T(128)}, f32[4096,1024]{1,0:T(8,128)}, f32[5632,1024]{1,0:T(8,128)}, f32[2816,1024]{1,0:T(8,128)}, f32[2048]{0:T(1024)}, /*index=5*/f32[2,57...) while((s32[]{:T(128)}, f32[4096,1024]{1,0:T(8,128)}, ...), condition=%wide.region_18.19_spmd.clone, body=%wide.region_0.18_spmd.clone.sunk | while | flops 45746876416 | bytes 740799360 | solution.py:314
  14.2 42.5 %all-reduce.4 = bf16[2048]{0:T(1024)(128)(2,1)S(1)} all-reduce(bf16[2048]{0:T(1024)(128)(2,1)S(1)} %dynamic-update-slice.3), channel_id=1, replica_groups=mesh['dp'=16,'fsdp'=2] {'dp','fsdp'}, use_global_device_ids=true, to_apply=%add | all-reduce | flops 2048 | bytes 8192 | tf_op jit(solution)/shard_map/while
  58.4 39.4 %all-gather.14.cloned.1.call-done = bf16[4096,1024]{1,0:T(8,128)(2,1)} async-done(((bf16[128,1024]{1,0:T(8,128)(2,1)}), bf16[4096,1024]{1,0:T(8,128)(2,1)}) %all-gather.14.cloned.1.call-update) | async-done | bytes 8388624 | tf_op jit(solution)/shard_map/while/body/eval_jaxpr/all_gather | solution.py:298
  120.1 10.7 all-gather.18.cloned.1.call-done
  136.4 59.3 %while.74 = (s32[]{:T(128)}, bf16[8,576,128]{1,2,0:T(8,128)(2,1)}, f32[8,2,576]{2,1,0:T(2,128)}, bf16[8,1152,128]{1,2,0:T(8,128)(2,1)S(1)}, bf16[8,576,128]{1,2,...) while((s32[]{:T(128)}, bf16[8,576,128]{1,2,0:T(8,128)(2,1)}, ...), condition=%wide.region_7.7_spmd.clone, body=%wide.region_4.6_spmd.clone.sunk | while | flops 349690752 | bytes 19968356 | solution.py:187
  200.8 25.8 %all-gather.20.cloned.1.call-done = bf16[1024,5632]{0,1:T(8,128)(2,1)} async-done(((bf16[1024,176]{0,1:T(8,128)(2,1)}), bf16[1024,5632]{0,1:T(8,128)(2,1)}) %all-gather.20.cloned.1.call-update) | async-done | bytes 11534352 | tf_op jit(solution)/shard_map/while/body/eval_jaxpr/all_gather | solution.py:299
  226.7 13.3 fusion.176
  239.9 55.7 %all-gather.22.cloned.1.call-done = bf16[2816,1024]{1,0:T(8,128)(2,1)} async-done(((bf16[88,1024]{1,0:T(8,128)(2,1)}), bf16[2816,1024]{1,0:T(8,128)(2,1)}) %all-gather.22.cloned.1.call-update) | async-done | bytes 5767184 | tf_op jit(solution)/shard_map/while/body/eval_jaxpr/all_gather | solution.py:307
  295.6 16.1 fusion.177
  311.7 13.0 multiply_reduce_fusion.12
  332.6 90.7 %while.75 = (s32[]{:T(128)}, bf16[8,576,128]{1,2,0:T(8,128)(2,1)}, bf16[8,1152,128]{1,2,0:T(8,128)(2,1)}, bf16[8,1152,128]{1,2,0:T(8,128)(2,1)}, bf16[8,1152,128...) while((s32[]{:T(128)}, bf16[8,576,128]{1,2,0:T(8,128)(2,1)}, ...), condition=%wide.region_12.12_spmd.clone, body=%wide.region_10.11_spmd.clone.sunk | while | flops 860625792 | bytes 46643592 | solution.py:247
  456.4 16.1 select_add_fusion.4
  492.5 10.9 bitcast_add_fusion.2
  508.0 40.3 %all-reduce.4 = bf16[2048]{0:T(1024)(128)(2,1)S(1)} all-reduce(bf16[2048]{0:T(1024)(128)(2,1)S(1)} %dynamic-update-slice.3), channel_id=1, replica_groups=mesh['dp'=16,'fsdp'=2] {'dp','fsdp'}, use_global_device_ids=true, to_apply=%add | all-reduce | flops 2048 | bytes 8192 | tf_op jit(solution)/shard_map/while
  549.9 38.0 %all-gather.14.cloned.1.call-done = bf16[4096,1024]{1,0:T(8,128)(2,1)} async-done(((bf16[128,1024]{1,0:T(8,128)(2,1)}), bf16[4096,1024]{1,0:T(8,128)(2,1)}) %all-gather.14.cloned.1.call-update) | async-done | bytes 8388624 | tf_op jit(solution)/shard_map/while/body/eval_jaxpr/all_gather | solution.py:298
  626.3 59.3 %while.74 = (s32[]{:T(128)}, bf16[8,576,128]{1,2,0:T(8,128)(2,1)}, f32[8,2,576]{2,1,0:T(2,128)}, bf16[8,1152,128]{1,2,0:T(8,128)(2,1)S(1)}, bf16[8,576,128]{1,2,...) while((s32[]{:T(128)}, bf16[8,576,128]{1,2,0:T(8,128)(2,1)}, ...), condition=%wide.region_7.7_spmd.clone, body=%wide.region_4.6_spmd.clone.sunk | while | flops 349690752 | bytes 19968356 | solution.py:187
  690.8 25.9 %all-gather.20.cloned.1.call-done = bf16[1024,5632]{0,1:T(8,128)(2,1)} async-done(((bf16[1024,176]{0,1:T(8,128)(2,1)}), bf16[1024,5632]{0,1:T(8,128)(2,1)}) %all-gather.20.cloned.1.call-update) | async-done | bytes 11534352 | tf_op jit(solution)/shard_map/while/body/eval_jaxpr/all_gather | solution.py:299
  716.7 13.3 fusion.176
  730.0 55.6 %all-gather.22.cloned.1.call-done = bf16[2816,1024]{1,0:T(8,128)(2,1)} async-done(((bf16[88,1024]{1,0:T(8,128)(2,1)}), bf16[2816,1024]{1,0:T(8,128)(2,1)}) %all-gather.22.cloned.1.call-update) | async-done | bytes 5767184 | tf_op jit(solution)/shard_map/while/body/eval_jaxpr/all_gather | solution.py:307
  785.6 16.4 fusion.177
  802.1 13.0 multiply_reduce_fusion.12
  823.0 90.6 %while.75 = (s32[]{:T(128)}, bf16[8,576,128]{1,2,0:T(8,128)(2,1)}, bf16[8,1152,128]{1,2,0:T(8,128)(2,1)}, bf16[8,1152,128]{1,2,0:T(8,128)(2,1)}, bf16[8,1152,128...) while((s32[]{:T(128)}, bf16[8,576,128]{1,2,0:T(8,128)(2,1)}, ...), condition=%wide.region_12.12_spmd.clone, body=%wide.region_10.11_spmd.clone.sunk | while | flops 860625792 | bytes 46643592 | solution.py:247
  949.3 22.0 %select_add_fusion.4 = f32[5632,1024]{1,0:T(8,128)} fusion(f32[5632,1024]{1,0:T(8,128)} %get-tuple-element.887, pred[]{:T(512)S(6)} %compare.3, bf16[576,2816]{1,0:T(8,128)(2,1)} %copy-done.44, bf16[576,2816]{1,0:T(8,128)(2,1)} %copy-done.43, f32[576,1024]{1,0:T(8,128)S(1)} %copy-done.6, f32[1024]{0:T(1024)S(1)} %get-tuple-element.758, ...), kind=kOutput, calls=%fused_computation.27.clone.1 | convolution fusion | flops 6670057472 | bytes 54991104 | tf_op jit(solution)/shard_map/while/body/eval_jaxpr/dot_general | solution.py:50
  991.3 14.0 bitcast_add_fusion.2
  1011.8 13.3 reshape.263
  1025.1 18.0 %reshape.261 = f32[32768,128]{1,0:T(8,128)} reshape(f32[4096,1024]{1,0:T(8,128)} %get-tuple-element.288) | data formatting | bytes 33554432 | tf_op jit(solution)/shard_map/reshape | solution.py:71
  1043.3 24.6 %reshape.262 = f32[45056,128]{1,0:T(8,128)} reshape(f32[5632,1024]{1,0:T(8,128)} %get-tuple-element.289) | data formatting | bytes 46137344 | tf_op jit(solution)/shard_map/reshape | solution.py:72
  1068.6 42.6 %all-reduce.2 = f32[2048]{0:T(1024)S(1)} all-reduce(f32[2048]{0:T(1024)S(1)} %copy-done.34), channel_id=9, replica_groups=mesh['dp'=16,'fsdp'=2] {'dp','fsdp'}, use_global_device_ids=true, to_apply=%region_25.26.clone | all-reduce | flops 2048 | bytes 16384
  1111.9 67.2 %reduce-scatter.10.cloned.1.call-done = f32[704,128]{1,0:T(8,128)} async-done(((f32[22528,128]{1,0:T(8,128)}), f32[704,128]{1,0:T(8,128)}) %reduce-scatter.10.cloned.1.call-update) | async-done | bytes 360464 | tf_op jit(solution)/shard_map/reduce_scatter | solution.py:321
  1180.7 179.3 %reduce-scatter.6.cloned.1.call-done = f32[1024,128]{1,0:T(8,128)} async-done(((f32[32768,128]{1,0:T(8,128)}), f32[1024,128]{1,0:T(8,128)}) %reduce-scatter.6.cloned.1.call-update) | async-done | bytes 524304 | tf_op jit(solution)/shard_map/reduce_scatter | solution.py:319
  1361.8 248.3 %reduce-scatter.8.cloned.1.call-done = f32[1408,128]{1,0:T(8,128)} async-done(((f32[45056,128]{1,0:T(8,128)}), f32[1408,128]{1,0:T(8,128)}) %reduce-scatter.8.cloned.1.call-update) | async-done | bytes 720912 | tf_op jit(solution)/shard_map/reduce_scatter | solution.py:320
  1619.8 44.5 %psum.15 = f32[]{:T(128)} all-reduce(f32[]{:T(128)} %psum.14), channel_id=1, replica_groups=mesh['dp'=16,'fsdp'=2] {'dp'}, use_global_device_ids=true, to_apply=%region_28.29 | all-reduce | flops 1 | bytes 8 | tf_op jit(solution)/shard_map/psum | solution.py:331
  (650 shorter events, 535.5 us)
Async XLA Ops:
  12.5 88.7 %copy-start.10 = (bf16[1024,176]{0,1:T(8,128)(2,1)}, bf16[1024,176]{0,1:T(8,128)(2,1)S(1)}, u32[]{:S(2)}) copy-start(bf16[1024,176]{0,1:T(8,128)(2,1)S(1)} %get-tuple-element.921) | copy-start | bytes 1081348 | tf_op jit(solution)/shard_map/while
  12.5 88.7 %copy-start.14 = (bf16[88,1024]{1,0:T(8,128)(2,1)}, bf16[88,1024]{1,0:T(8,128)(2,1)S(1)}, u32[]{:S(2)}) copy-start(bf16[88,1024]{1,0:T(8,128)(2,1)S(1)} %get-tuple-element.922) | copy-start | bytes 540676 | tf_op jit(solution)/shard_map/while
  12.5 85.2 %all-gather.14.cloned.1.call-start = ((), (), s32[]{:S(2)}) async-start(), calls=%async_computation.8 | async-start | bytes 8650752 | tf_op jit(solution)/shard_map/while/body/eval_jaxpr/all_gather | solution.py:298
  13.3 103.9 %all-gather.16.cloned.1.call-start = ((), (), s32[]{:S(2)}) async-start(), calls=%async_computation.9 | async-start | bytes 3538944 | tf_op jit(solution)/shard_map/while/body/eval_jaxpr/all_gather | solution.py:185
  58.3 42.9 %copy-start.20 = (f32[576]{0:T(1024)}, f32[576]{0:T(1024)S(1)}, u32[]{:S(2)}) copy-start(f32[576]{0:T(1024)S(1)} %fusion.171) | copy-start | bytes 6916 | tf_op jit(solution)/shard_map/while
  58.3 42.9 %copy-start.28 = (f32[576]{0:T(1024)}, f32[576]{0:T(1024)S(1)}, u32[]{:S(2)}) copy-start(f32[576]{0:T(1024)S(1)} %fusion.172) | copy-start | bytes 6916 | tf_op jit(solution)/shard_map/while
  58.4 42.9 %copy-start.26 = (f32[1024]{0:T(1024)}, f32[1024]{0:T(1024)S(1)}, u32[]{:S(2)}) copy-start(f32[1024]{0:T(1024)S(1)} %get-tuple-element.750) | copy-start | bytes 12292 | tf_op jit(solution)/shard_map/while
  58.4 42.9 %copy-start.3 = (bf16[2,576,1024]{2,1,0:T(8,128)(2,1)S(1)}, bf16[2,576,1024]{2,1,0:T(8,128)(2,1)}, u32[]{:S(2)}) copy-start(bf16[2,576,1024]{2,1,0:T(8,128)(2,1)} %get-tuple-element.915) | copy-start | bytes 7077892 | tf_op jit(solution)/shard_map/while
  107.4 23.4 %all-gather.18.cloned.1.call-start = ((), (), s32[]{:S(2)}) async-start(), calls=%async_computation.10 | async-start | bytes 3538944 | tf_op jit(solution)/shard_map/while/body/eval_jaxpr/all_gather | solution.py:184
  108.2 118.5 %all-gather.20.cloned.1.call-start = ((), (), s32[]{:S(2)}) async-start(), calls=%async_computation.11 | async-start | bytes 11894784 | tf_op jit(solution)/shard_map/while/body/eval_jaxpr/all_gather | solution.py:299
  108.7 186.9 %all-gather.22.cloned.1.call-start = ((), (), s32[]{:S(2)}) async-start(), calls=%async_computation.12 | async-start | bytes 5947392 | tf_op jit(solution)/shard_map/while/body/eval_jaxpr/all_gather | solution.py:307
  109.3 363.2 %reduce-scatter.12.cloned.1.call-start = ((), (), s32[]{:S(2)}) async-start(), calls=%async_computation.13 | async-start | bytes 3538944 | tf_op jit(solution)/shard_map/while/body/eval_jaxpr/reduce_scatter | solution.py:263
  200.8 124.0 %copy-start.30 = (f32[576]{0:T(1024)}, f32[576]{0:T(1024)S(1)}, u32[]{:S(2)}) copy-start(f32[576]{0:T(1024)S(1)} %fusion.175) | copy-start | bytes 6916 | tf_op jit(solution)/shard_map/while
  427.6 44.9 %reduce-scatter.14.cloned.1.call-start = ((), (), s32[]{:S(2)}) async-start(), calls=%async_computation.14 | async-start | bytes 3538944 | tf_op jit(solution)/shard_map/while/body/eval_jaxpr/reduce_scatter | solution.py:260
  506.3 85.1 %copy-start.10 = (bf16[1024,176]{0,1:T(8,128)(2,1)}, bf16[1024,176]{0,1:T(8,128)(2,1)S(1)}, u32[]{:S(2)}) copy-start(bf16[1024,176]{0,1:T(8,128)(2,1)S(1)} %get-tuple-element.921) | copy-start | bytes 1081348 | tf_op jit(solution)/shard_map/while
  506.3 85.1 %copy-start.14 = (bf16[88,1024]{1,0:T(8,128)(2,1)}, bf16[88,1024]{1,0:T(8,128)(2,1)S(1)}, u32[]{:S(2)}) copy-start(bf16[88,1024]{1,0:T(8,128)(2,1)S(1)} %get-tuple-element.922) | copy-start | bytes 540676 | tf_op jit(solution)/shard_map/while
  506.3 81.6 %all-gather.14.cloned.1.call-start = ((), (), s32[]{:S(2)}) async-start(), calls=%async_computation.8 | async-start | bytes 8650752 | tf_op jit(solution)/shard_map/while/body/eval_jaxpr/all_gather | solution.py:298
  507.0 100.2 %all-gather.16.cloned.1.call-start = ((), (), s32[]{:S(2)}) async-start(), calls=%async_computation.9 | async-start | bytes 3538944 | tf_op jit(solution)/shard_map/while/body/eval_jaxpr/all_gather | solution.py:185
  549.8 41.5 %copy-start.20 = (f32[576]{0:T(1024)}, f32[576]{0:T(1024)S(1)}, u32[]{:S(2)}) copy-start(f32[576]{0:T(1024)S(1)} %fusion.171) | copy-start | bytes 6916 | tf_op jit(solution)/shard_map/while
  549.9 41.5 %copy-start.28 = (f32[576]{0:T(1024)}, f32[576]{0:T(1024)S(1)}, u32[]{:S(2)}) copy-start(f32[576]{0:T(1024)S(1)} %fusion.172) | copy-start | bytes 6916 | tf_op jit(solution)/shard_map/while
  549.9 41.5 %copy-start.26 = (f32[1024]{0:T(1024)}, f32[1024]{0:T(1024)S(1)}, u32[]{:S(2)}) copy-start(f32[1024]{0:T(1024)S(1)} %get-tuple-element.750) | copy-start | bytes 12292 | tf_op jit(solution)/shard_map/while
  597.5 23.3 %all-gather.18.cloned.1.call-start = ((), (), s32[]{:S(2)}) async-start(), calls=%async_computation.10 | async-start | bytes 3538944 | tf_op jit(solution)/shard_map/while/body/eval_jaxpr/all_gather | solution.py:184
  598.1 118.6 %all-gather.20.cloned.1.call-start = ((), (), s32[]{:S(2)}) async-start(), calls=%async_computation.11 | async-start | bytes 11894784 | tf_op jit(solution)/shard_map/while/body/eval_jaxpr/all_gather | solution.py:299
  598.9 186.8 %all-gather.22.cloned.1.call-start = ((), (), s32[]{:S(2)}) async-start(), calls=%async_computation.12 | async-start | bytes 5947392 | tf_op jit(solution)/shard_map/while/body/eval_jaxpr/all_gather | solution.py:307
  599.4 371.9 %reduce-scatter.12.cloned.1.call-start = ((), (), s32[]{:S(2)}) async-start(), calls=%async_computation.13 | async-start | bytes 3538944 | tf_op jit(solution)/shard_map/while/body/eval_jaxpr/reduce_scatter | solution.py:263
  690.8 124.3 %copy-start.30 = (f32[576]{0:T(1024)}, f32[576]{0:T(1024)S(1)}, u32[]{:S(2)}) copy-start(f32[576]{0:T(1024)S(1)} %fusion.175) | copy-start | bytes 6916 | tf_op jit(solution)/shard_map/while
  917.9 53.4 %reduce-scatter.14.cloned.1.call-start = ((), (), s32[]{:S(2)}) async-start(), calls=%async_computation.14 | async-start | bytes 3538944 | tf_op jit(solution)/shard_map/while/body/eval_jaxpr/reduce_scatter | solution.py:260
  1011.7 167.3 %reduce-scatter.10.cloned.1.call-start = ((), (), s32[]{:S(2)}) async-start(), calls=%async_computation.7 | async-start | bytes 11894784 | tf_op jit(solution)/shard_map/reduce_scatter | solution.py:321
  1025.1 335.0 %reduce-scatter.6.cloned.1.call-start = ((), (), s32[]{:S(2)}) async-start(), calls=%async_computation.5 | async-start | bytes 17301504 | tf_op jit(solution)/shard_map/reduce_scatter | solution.py:319
  1043.2 566.9 %reduce-scatter.8.cloned.1.call-start = ((), (), s32[]{:S(2)}) async-start(), calls=%async_computation.6 | async-start | bytes 23789568 | tf_op jit(solution)/shard_map/reduce_scatter | solution.py:320
  1361.8 305.2 %copy-start.19 = (f32[1024,128]{1,0:T(8,128)S(1)}, f32[1024,128]{1,0:T(8,128)}, u32[]{:S(2)}) copy-start(f32[1024,128]{1,0:T(8,128)} %reduce-scatter.6.cloned.1.call-done) | copy-start | bytes 1572868
  1610.2 56.7 %copy-start.17 = (f32[1408,128]{1,0:T(8,128)S(1)}, f32[1408,128]{1,0:T(8,128)}, u32[]{:S(2)}) copy-start(f32[1408,128]{1,0:T(8,128)} %reduce-scatter.8.cloned.1.call-done) | copy-start | bytes 2162692
  (63 other events, 467.0 us)
Sparse Core Ops, SparseCore 0:
  16.8 80.9 all-gather.13
  107.5 9.5 all-gather.15
  118.7 12.1 all-gather.17
  134.1 92.5 all-gather.19
  229.9 65.6 all-gather.21
  427.7 8.8 reduce-scatter.11
  439.0 11.0 reduce-scatter.13
  510.6 77.2 all-gather.13
  597.6 9.5 all-gather.15
  608.6 12.1 all-gather.17
  624.2 92.4 all-gather.19
  720.0 65.5 all-gather.21
  918.0 8.8 reduce-scatter.11
  929.1 11.0 reduce-scatter.13
Sparse Core Ops, SparseCore 1:
  1025.2 153.8 reduce-scatter.9
  1181.2 178.8 reduce-scatter.5
  1362.2 247.9 reduce-scatter.7
